TPU v7x, 32 devices: a whole 2x2x4 slice. The times are simulated.
32 devices in a mesh: seq: 8 (over z, core), tp: 4 (over y, x).
Axes of the slice: x: 2, y: 2, z: 4, core: 2. Of those that a mesh axis runs over, the one named last changes fastest.
Arguments:
- layer_in: bfloat16 [4096, 2048], P('seq'), may hold values from -6 to 6
- positions: int32 [4096], P('seq'), may hold values from 0 to 2047, as said below
- seq_ids: int32 [4096], P('seq'), may hold values from 0 to 1, as said below
- norm1_gain: float32 [2048], replicated, may hold values from 0.5 to 1.5
- norm2_gain: float32 [2048], replicated, may hold values from 0.5 to 1.5
- w_query: float32 [2048, 2048], P('seq', 'tp'), may hold values from -0.125 to 0.125
- w_key: float32 [2048, 2048], P('seq', 'tp'), may hold values from -0.125 to 0.125
- w_value: float32 [2048, 2048], P('seq', 'tp'), may hold values from -0.125 to 0.125
- w_out: float32 [2048, 2048], P('tp', 'seq'), may hold values from -4 to 4
- w_gate: float32 [2048, 8192], P('seq', 'tp'), may hold values from -0.125 to 0.125
- w_up: float32 [2048, 8192], P('seq', 'tp'), may hold values from -0.125 to 0.125
- w_down: float32 [8192, 2048], P('tp', 'seq'), may hold values from -0.0625 to 0.0625
- out_grad: bfloat16 [4096, 2048], P('seq'), may hold values from -6 to 6
Outputs:
- layer_out: bfloat16 [4096, 2048], P('seq')
- in_grad: float32 [4096, 2048], P('seq')
- grad_norm1: float32 [2048], P('seq')
- grad_norm2: float32 [2048], P('seq')
- grad_w_query: float32 [2048, 2048], P('seq', 'tp')
- grad_w_key: float32 [2048, 2048], P('seq', 'tp')
- grad_w_value: float32 [2048, 2048], P('seq', 'tp')
- grad_w_out: float32 [2048, 2048], P('tp', 'seq')
- grad_w_gate: float32 [2048, 8192], P('seq', 'tp')
- grad_w_up: float32 [2048, 8192], P('seq', 'tp')
- grad_w_down: float32 [8192, 2048], P('tp', 'seq')
Inputs may be any that keep to these rules, and one draw needn't show every extreme that they name: The shard of 512 rows at index r of seq holds, in an order that varies from shard to shard, four blocks of 128 consecutive positions: for each of the two sequences its blocks number r and 15 - r. Each position of each sequence appears once. `seq_ids`: the sequence of each row, constant over each block of 128 rows described for positions; each shard holds two such blocks of each sequence, and each sequence has 2048 rows.
All inputs are finite; a program needn't handle non-finite values.
Results may differ from a plain program's by a relative error of at most 0.024.
Values may be sent and summed in bfloat16 or wider, within the bound.
No kernel may reach another device: no remote copies, remote signals or barrier semaphores. Data moves between devices by JAX's collectives and lax.ppermute only.
A program may use at most 192 MiB of HBM per device.

v0:
```python
import math
import jax
import jax.numpy as jnp
from jax import lax
from jax.sharding import PartitionSpec as P

HD = 128
EPSILON = 1e-06


def angles(places):
    half_width = HD // 2
    frequency = jnp.power(
        jnp.float32(10000.0), -jnp.arange(half_width, dtype=jnp.float32) / half_width
    )
    phase_angle = places.astype(jnp.float32)[:, None] * frequency[None, :]
    return (jnp.cos(phase_angle)[:, None, :], jnp.sin(phase_angle)[:, None, :])


def rotate(heads, rot_cos, rot_sin):
    half_width = heads.shape[-1] // 2
    front_half = heads[..., :half_width]
    back_half = heads[..., half_width:]
    return jnp.concatenate(
        [front_half * rot_cos - back_half * rot_sin, back_half * rot_cos + front_half * rot_sin],
        axis=-1,
    )


def rotate_back(grads, rot_cos, rot_sin):
    half_width = grads.shape[-1] // 2
    front_half = grads[..., :half_width]
    back_half = grads[..., half_width:]
    return jnp.concatenate(
        [front_half * rot_cos + back_half * rot_sin, back_half * rot_cos - front_half * rot_sin],
        axis=-1,
    )


def matrix(left, right):
    return jnp.dot(left, right, preferred_element_type=jnp.float32)


def inner_rows(left, right):
    return lax.dot_general(
        left, right, (((0,), (0,)), ((), ())), preferred_element_type=jnp.float32
    )


def outer_cols(left, right):
    return lax.dot_general(
        left, right, (((1,), (1,)), ((), ())), preferred_element_type=jnp.float32
    )


def arrange(values, order):
    blocks = values.reshape((4, values.shape[0] // 4) + values.shape[1:])
    return blocks[order].reshape(values.shape)


def regroup(values, shard_rows):
    count = values.shape[0] // shard_rows
    half_rows = shard_rows // 2
    split_form = values.reshape((count, 2, half_rows) + values.shape[1:])
    return jnp.swapaxes(split_form, 0, 1).reshape((2, count * half_rows) + values.shape[1:])


def unsplit(values):
    return values.reshape((values.shape[0] * values.shape[1],) + values.shape[2:])


def split_scores(query_split, key_split, qpos_split, kpos_split, score_scale, score_bias):
    raw = (
        jnp.einsum("sqhd,skhd->shqk", query_split, key_split, preferred_element_type=jnp.float32)
        * score_scale
        + score_bias
    )
    allowed = (kpos_split[:, None, :] <= qpos_split[:, :, None])[:, None]
    return (jax.nn.sigmoid(raw), allowed)


def split_attend(
    query_split, key_split, value_split, qpos_split, kpos_split, score_scale, score_bias
):
    sig, allowed = split_scores(
        query_split, key_split, qpos_split, kpos_split, score_scale, score_bias
    )
    attn_weights = jnp.where(allowed, sig, 0.0).astype(jnp.bfloat16)
    return unsplit(
        jnp.einsum("shqk,skhd->sqhd", attn_weights, value_split, preferred_element_type=jnp.float32)
    )


def split_grads(
    query_split, key_split, value_split, grad_split, qpos_split, kpos_split, score_scale, score_bias
):
    sig, allowed = split_scores(
        query_split, key_split, qpos_split, kpos_split, score_scale, score_bias
    )
    attn_weights = jnp.where(allowed, sig, 0.0).astype(jnp.bfloat16)
    grad_prob = jnp.einsum(
        "sqhd,skhd->shqk", grad_split, value_split, preferred_element_type=jnp.float32
    )
    grad_score = jnp.where(allowed, grad_prob * sig * (1.0 - sig), 0.0).astype(jnp.bfloat16)
    return (attn_weights, grad_score)


def on_device(
    layer_in,
    positions,
    seq_ids,
    norm1_gain,
    norm2_gain,
    w_query,
    w_key,
    w_value,
    w_out,
    w_gate,
    w_up,
    w_down,
    out_grad,
):
    row_count = layer_in.shape[0]
    shard_count = lax.axis_size("seq")
    score_bias = -math.log(shard_count * row_count // 2)
    score_scale = 1.0 / math.sqrt(HD)
    block_seq = seq_ids.reshape(4, row_count // 4)[:, 0]
    order = jnp.argsort(block_seq, stable=True)
    inverse = jnp.argsort(order, stable=True)
    pos_sorted = arrange(positions, order)
    seq_sorted = arrange(seq_ids, order)
    every_pos, every_seq = (
        lax.all_gather(pos_sorted, "seq", axis=0, tiled=True),
        lax.all_gather(seq_sorted, "seq", axis=0, tiled=True),
    )
    query_full, key_full, value_full, out_full, gate_full, up_full, down_full = (
        lax.all_gather(w_query.astype(jnp.bfloat16), "seq", axis=0, tiled=True),
        lax.all_gather(w_key.astype(jnp.bfloat16), "seq", axis=0, tiled=True),
        lax.all_gather(w_value.astype(jnp.bfloat16), "seq", axis=0, tiled=True),
        lax.all_gather(w_out.astype(jnp.bfloat16), "seq", axis=1, tiled=True),
        lax.all_gather(w_gate.astype(jnp.bfloat16), "seq", axis=0, tiled=True),
        lax.all_gather(w_up.astype(jnp.bfloat16), "seq", axis=0, tiled=True),
        lax.all_gather(w_down.astype(jnp.bfloat16), "seq", axis=1, tiled=True),
    )
    head_cols = query_full.shape[1]
    head_count = head_cols // HD
    rot_cos, rot_sin = angles(positions)
    inputs = layer_in.astype(jnp.float32)
    scale_one = lax.rsqrt(jnp.mean(inputs * inputs, axis=-1, keepdims=True) + EPSILON)
    normed_one = (inputs * scale_one * norm1_gain).astype(jnp.bfloat16)
    query_heads = rotate(
        matrix(normed_one, query_full).reshape(row_count, head_count, HD), rot_cos, rot_sin
    ).astype(jnp.bfloat16)
    key_heads = rotate(
        matrix(normed_one, key_full).reshape(row_count, head_count, HD), rot_cos, rot_sin
    ).astype(jnp.bfloat16)
    value_rows = matrix(normed_one, value_full).astype(jnp.bfloat16)
    query_sorted = arrange(query_heads, order)
    key_rows = arrange(key_heads.reshape(row_count, head_cols), order)
    value_sorted = arrange(value_rows, order)
    query_split = regroup(query_sorted, row_count)
    qpos_split = regroup(pos_sorted, row_count)
    zero_out = jnp.zeros((row_count, head_count, HD), jnp.float32)
    key_block = lax.all_gather(key_rows, "seq", axis=0, tiled=True)
    value_block = lax.all_gather(value_sorted, "seq", axis=0, tiled=True)
    piece_rows = key_block.shape[0]
    key_pos = every_pos
    key_heads_piece = key_block.reshape(piece_rows, head_count, HD)
    value_heads_piece = value_block.reshape(piece_rows, head_count, HD)
    term = split_attend(
        query_split,
        regroup(key_heads_piece, row_count),
        regroup(value_heads_piece, row_count),
        qpos_split,
        regroup(key_pos, row_count),
        score_scale,
        score_bias,
    )
    mixed_heads = arrange(term, inverse).reshape(row_count, head_cols).astype(jnp.bfloat16)
    residual = inputs + lax.psum(matrix(mixed_heads, out_full), "tp")
    scale_two = lax.rsqrt(jnp.mean(residual * residual, axis=-1, keepdims=True) + EPSILON)
    normed_two = (residual * scale_two * norm2_gain).astype(jnp.bfloat16)
    gate = matrix(normed_two, gate_full)
    up_proj = matrix(normed_two, up_full)
    gate_sig = jax.nn.sigmoid(gate)
    hidden = (gate * gate_sig * up_proj).astype(jnp.bfloat16)
    layer_out = (
        residual
        + lax.psum(matrix(hidden, down_full).astype(jnp.bfloat16), "tp").astype(jnp.float32)
    ).astype(jnp.bfloat16)
    query_full, key_full, value_full, out_full, gate_full, up_full, down_full = (
        lax.all_gather(w_query.astype(jnp.bfloat16), "seq", axis=0, tiled=True),
        lax.all_gather(w_key.astype(jnp.bfloat16), "seq", axis=0, tiled=True),
        lax.all_gather(w_value.astype(jnp.bfloat16), "seq", axis=0, tiled=True),
        lax.all_gather(w_out.astype(jnp.bfloat16), "seq", axis=1, tiled=True),
        lax.all_gather(w_gate.astype(jnp.bfloat16), "seq", axis=0, tiled=True),
        lax.all_gather(w_up.astype(jnp.bfloat16), "seq", axis=0, tiled=True),
        lax.all_gather(w_down.astype(jnp.bfloat16), "seq", axis=1, tiled=True),
    )
    grad_w_down = inner_rows(hidden, out_grad)
    grad_hidden = outer_cols(out_grad, down_full)
    grad_gate = (grad_hidden * up_proj * gate_sig * (1.0 + gate * (1.0 - gate_sig))).astype(
        jnp.bfloat16
    )
    grad_up = (grad_hidden * gate * gate_sig).astype(jnp.bfloat16)
    grad_w_gate = inner_rows(normed_two, grad_gate)
    grad_w_up = inner_rows(normed_two, grad_up)
    grad_normed_two = lax.psum(
        (outer_cols(grad_gate, gate_full) + outer_cols(grad_up, up_full)).astype(jnp.bfloat16), "tp"
    ).astype(jnp.float32)
    gain_two = jnp.sum(grad_normed_two * residual * scale_two, axis=0)
    effect_two = grad_normed_two * norm2_gain
    grad_resid = (
        out_grad.astype(jnp.float32)
        + scale_two * effect_two
        - residual
        * (scale_two * scale_two * scale_two)
        * jnp.mean(effect_two * residual, axis=-1, keepdims=True)
    )
    grad_resid_low = grad_resid.astype(jnp.bfloat16)
    grad_w_out = inner_rows(mixed_heads, grad_resid_low)
    grad_mixed = (
        outer_cols(grad_resid_low, out_full).astype(jnp.bfloat16).reshape(row_count, head_count, HD)
    )
    grad_sorted = arrange(grad_mixed, order)
    grad_split = regroup(grad_sorted, row_count)
    all_keys, all_values = (
        lax.all_gather(key_rows, "seq", axis=0, tiled=True),
        lax.all_gather(value_sorted, "seq", axis=0, tiled=True),
    )
    key_stack = all_keys.reshape(shard_count, row_count, head_count, HD)
    value_stack = all_values.reshape(shard_count, row_count, head_count, HD)
    kpos_stack = every_pos.reshape(shard_count, row_count)

    def back_step(grad_query, blocks):
        key_block, value_block, key_pos = blocks
        key_split = regroup(key_block, row_count)
        attn_weights, grad_score = split_grads(
            query_split,
            key_split,
            regroup(value_block, row_count),
            grad_split,
            qpos_split,
            regroup(key_pos, row_count),
            score_scale,
            score_bias,
        )
        grad_query = (
            grad_query
            + unsplit(
                jnp.einsum(
                    "shqk,skhd->sqhd", grad_score, key_split, preferred_element_type=jnp.float32
                )
            )
            * score_scale
        )
        key_term = (
            jnp.einsum(
                "shqk,sqhd->skhd", grad_score, query_split, preferred_element_type=jnp.float32
            )
            * score_scale
        )
        value_term = jnp.einsum(
            "shqk,sqhd->skhd", attn_weights, grad_split, preferred_element_type=jnp.float32
        )
        half_rows = row_count // 2
        key_back = jnp.swapaxes(key_term.reshape(2, 1, half_rows, head_cols), 0, 1).reshape(
            row_count, head_cols
        )
        value_back = jnp.swapaxes(value_term.reshape(2, 1, half_rows, head_cols), 0, 1).reshape(
            row_count, head_cols
        )
        return (grad_query, (key_back, value_back))

    grad_query, term_stack = lax.scan(back_step, zero_out, (key_stack, value_stack, kpos_stack))
    key_terms = term_stack[0].reshape(shard_count * row_count, head_cols)
    value_terms = term_stack[1].reshape(shard_count * row_count, head_cols)
    key_sum, value_sum = (
        lax.psum_scatter(
            key_terms.astype(jnp.bfloat16), "seq", scatter_dimension=0, tiled=True
        ).astype(jnp.float32),
        lax.psum_scatter(
            value_terms.astype(jnp.bfloat16), "seq", scatter_dimension=0, tiled=True
        ).astype(jnp.float32),
    )
    grad_query = arrange(grad_query, inverse)
    key_sum = arrange(key_sum, inverse)
    value_sum = arrange(value_sum, inverse)
    grad_query_lin = (
        rotate_back(grad_query, rot_cos, rot_sin).reshape(row_count, head_cols).astype(jnp.bfloat16)
    )
    grad_key_lin = (
        rotate_back(key_sum.reshape(row_count, head_count, HD), rot_cos, rot_sin)
        .reshape(row_count, head_cols)
        .astype(jnp.bfloat16)
    )
    grad_value_low = value_sum.astype(jnp.bfloat16)
    grad_w_query = inner_rows(normed_one, grad_query_lin)
    grad_w_key = inner_rows(normed_one, grad_key_lin)
    grad_w_value = inner_rows(normed_one, grad_value_low)
    grad_normed_one = lax.psum(
        (
            outer_cols(grad_query_lin, query_full)
            + outer_cols(grad_key_lin, key_full)
            + outer_cols(grad_value_low, value_full)
        ).astype(jnp.bfloat16),
        "tp",
    ).astype(jnp.float32)
    gain_one = jnp.sum(grad_normed_one * inputs * scale_one, axis=0)
    effect_one = grad_normed_one * norm1_gain
    in_grad = (
        grad_resid
        + scale_one * effect_one
        - inputs
        * (scale_one * scale_one * scale_one)
        * jnp.mean(effect_one * inputs, axis=-1, keepdims=True)
    )
    summed = (
        lax.psum_scatter(
            grad_w_query.astype(jnp.bfloat16), "seq", scatter_dimension=0, tiled=True
        ).astype(jnp.float32),
        lax.psum_scatter(
            grad_w_key.astype(jnp.bfloat16), "seq", scatter_dimension=0, tiled=True
        ).astype(jnp.float32),
        lax.psum_scatter(
            grad_w_value.astype(jnp.bfloat16), "seq", scatter_dimension=0, tiled=True
        ).astype(jnp.float32),
        lax.psum_scatter(
            grad_w_out.astype(jnp.bfloat16), "seq", scatter_dimension=1, tiled=True
        ).astype(jnp.float32),
        lax.psum_scatter(
            grad_w_gate.astype(jnp.bfloat16), "seq", scatter_dimension=0, tiled=True
        ).astype(jnp.float32),
        lax.psum_scatter(
            grad_w_up.astype(jnp.bfloat16), "seq", scatter_dimension=0, tiled=True
        ).astype(jnp.float32),
        lax.psum_scatter(
            grad_w_down.astype(jnp.bfloat16), "seq", scatter_dimension=1, tiled=True
        ).astype(jnp.float32),
        lax.psum_scatter(
            gain_one.astype(jnp.bfloat16), "seq", scatter_dimension=0, tiled=True
        ).astype(jnp.float32),
        lax.psum_scatter(
            gain_two.astype(jnp.bfloat16), "seq", scatter_dimension=0, tiled=True
        ).astype(jnp.float32),
    )
    return (
        layer_out,
        in_grad,
        summed[7],
        summed[8],
        summed[0],
        summed[1],
        summed[2],
        summed[3],
        summed[4],
        summed[5],
        summed[6],
    )


def solution(mesh):
    in_specs = (
        P("seq", None),
        P("seq"),
        P("seq"),
        P(),
        P(),
        P("seq", "tp"),
        P("seq", "tp"),
        P("seq", "tp"),
        P("tp", "seq"),
        P("seq", "tp"),
        P("seq", "tp"),
        P("tp", "seq"),
        P("seq", None),
    )
    out_specs = (
        P("seq", None),
        P("seq", None),
        P("seq"),
        P("seq"),
        P("seq", "tp"),
        P("seq", "tp"),
        P("seq", "tp"),
        P("tp", "seq"),
        P("seq", "tp"),
        P("seq", "tp"),
        P("tp", "seq"),
    )
    return jax.shard_map(
        on_device, mesh=mesh, in_specs=in_specs, out_specs=out_specs, check_vma=False
    )
```

profile of v0, /device:TPU:0, one launch (start us, length us, event | category | flops | bytes accessed | tf_op | source)
XLA Modules:
  0.0 1521.6 jit_solution(15668812939216227215)
XLA Ops:
  16.8 25.2 %all-gather.17.cloned.1.call-done = bf16[2048,512]{1,0:T(8,128)(2,1)} async-done(((bf16[256,512]{1,0:T(8,128)(2,1)}), bf16[2048,512]{1,0:T(8,128)(2,1)}) %all-gather.17.cloned.1.call-update) | async-done | bytes 2097168 | tf_op jit(solution)/shard_map/all_gather | solution.py:138
  42.0 3.0 fusion.50
  45.0 27.8 %all-gather.15.cloned.1.call-done = bf16[2048,512]{1,0:T(8,128)(2,1)} async-done(((bf16[256,512]{1,0:T(8,128)(2,1)}), bf16[2048,512]{1,0:T(8,128)(2,1)}) %all-gather.15.cloned.1.call-update) | async-done | bytes 2097168 | tf_op jit(solution)/shard_map/all_gather | solution.py:137
  72.8 3.0 fusion.52
  79.1 24.5 %all-gather.11.cloned.1.call-done = bf16[2048,512]{1,0:T(8,128)(2,1)} async-done(((bf16[256,512]{1,0:T(8,128)(2,1)}), bf16[2048,512]{1,0:T(8,128)(2,1)}) %all-gather.11.cloned.1.call-update) | async-done | bytes 2097168 | tf_op jit(solution)/shard_map/all_gather | solution.py:139
  103.7 3.7 convolution_convert_fusion.9
  112.6 13.4 all-gather
  132.0 20.4 %all-gather.19.cloned.1.call-done = bf16[4096,512]{0,1:T(8,128)(2,1)} async-done(((bf16[512,512]{0,1:T(8,128)(2,1)}), bf16[4096,512]{0,1:T(8,128)(2,1)}) %all-gather.19.cloned.1.call-update) | async-done | bytes 4194320 | tf_op jit(solution)/shard_map/all_gather | solution.py:164
  152.4 7.8 reshape.326
  160.2 11.8 copy.119
  172.0 5.2 copy.100
  177.3 23.2 %all-gather.13.cloned.1.call-done = bf16[4096,512]{0,1:T(8,128)(2,1)} async-done(((bf16[512,512]{0,1:T(8,128)(2,1)}), bf16[4096,512]{0,1:T(8,128)(2,1)}) %all-gather.13.cloned.1.call-update) | async-done | bytes 4194320 | tf_op jit(solution)/shard_map/all_gather | solution.py:165
  200.4 7.8 reshape.324
  208.2 11.8 copy.117
  220.0 6.1 copy.93
  226.1 7.4 reshape.215
  233.6 10.7 fusion.33
  248.5 5.0 fusion.37
  256.4 2.9 convert_element_type.200
  262.3 94.0 %all-reduce.8.cloned.1.call-done = f32[512,2048]{1,0:T(8,128)} async-done(((f32[512,2048]{1,0:T(8,128)}), f32[512,2048]{1,0:T(8,128)}) %all-reduce.8.cloned.1.call-update) | async-done | bytes 4194320 | tf_op jit(solution)/shard_map/psum | solution.py:180
  361.6 79.1 %all-gather.23.cloned.1.call-done = bf16[2048,2048]{1,0:T(8,128)(2,1)} async-done(((bf16[256,2048]{1,0:T(8,128)(2,1)}), bf16[2048,2048]{1,0:T(8,128)(2,1)}) %all-gather.23.cloned.1.call-update) | async-done | bytes 8388624 | tf_op jit(solution)/shard_map/all_gather | solution.py:141
  440.6 9.4 fusion.56
  450.0 73.5 %all-gather.25.cloned.1.call-done = bf16[2048,2048]{1,0:T(8,128)(2,1)} async-done(((bf16[256,2048]{1,0:T(8,128)(2,1)}), bf16[2048,2048]{1,0:T(8,128)(2,1)}) %all-gather.25.cloned.1.call-update) | async-done | bytes 8388624 | tf_op jit(solution)/shard_map/all_gather | solution.py:142
  523.5 9.4 fusion.57
  532.9 73.7 %all-gather.27.cloned.1.call-done = bf16[2048,2048]{1,0:T(8,128)(2,1)} async-done(((bf16[2048,256]{1,0:T(8,128)(2,1)}), bf16[2048,2048]{1,0:T(8,128)(2,1)}) %all-gather.27.cloned.1.call-update) | async-done | bytes 8388624 | tf_op jit(solution)/shard_map/all_gather | solution.py:143
  606.7 11.8 multiply_convert_fusion
  618.5 8.5 fusion.58
  627.0 5.8 add_convert_fusion.1
  633.8 6.3 copy.125
  640.1 8.1 copy.106
  648.2 6.4 copy.126
  654.6 8.0 copy.107
  662.7 38.2 %all-reduce.10.cloned.1.call-done = bf16[512,2048]{1,0:T(8,128)(2,1)} async-done(((bf16[512,2048]{1,0:T(8,128)(2,1)}), bf16[512,2048]{1,0:T(8,128)(2,1)}) %all-reduce.10.cloned.1.call-update) | async-done | bytes 2097168 | tf_op jit(solution)/shard_map/psum | solution.py:208
  700.8 4.3 fusion.23
  711.9 172.8 %while.16 = (s32[]{:T(128)}, f32[512,4,128]{2,0,1:T(8,128)}, bf16[8,512,512]{2,1,0:T(8,128)(2,1)}, bf16[8,512,512]{2,1,0:T(8,128)(2,1)}, bf16[8,512,4,128]{3,1,2...) while((s32[]{:T(128)}, f32[512,4,128]{2,0,1:T(8,128)}, ...), condition=%wide.wide.region_9.10_spmd.clone, body=%wide.wide.region_8.9_spmd.clone.sunk | while | flops 678297600 | bytes 37630664 | solution.py:275
  713.8 3.1 add_divide_fusion.4
  734.3 3.1 add_divide_fusion.4
  756.0 3.1 add_divide_fusion.4
  777.7 3.1 add_divide_fusion.4
  799.5 3.1 add_divide_fusion.4
  821.2 3.1 add_divide_fusion.4
  843.0 3.1 add_divide_fusion.4
  864.7 3.1 add_divide_fusion.4
  885.9 4.8 convolution_convert_fusion.3
  892.3 42.6 %reduce-scatter.10.cloned.1.call-done = bf16[512,512]{1,0:T(8,128)(2,1)} async-done(((bf16[4096,512]{1,0:T(8,128)(2,1)}), bf16[512,512]{1,0:T(8,128)(2,1)}) %reduce-scatter.10.cloned.1.call-update) | async-done | bytes 524304 | tf_op jit(solution)/shard_map/reduce_scatter | solution.py:279
  945.5 2.8 convolution_convert_fusion.6
  948.4 2.8 convolution_convert_fusion.5
  951.3 34.1 %reduce-scatter.12.cloned.1.call-done = bf16[512,512]{1,0:T(8,128)(2,1)} async-done(((bf16[4096,512]{1,0:T(8,128)(2,1)}), bf16[512,512]{1,0:T(8,128)(2,1)}) %reduce-scatter.12.cloned.1.call-update) | async-done | bytes 524304 | tf_op jit(solution)/shard_map/reduce_scatter | solution.py:282
  987.8 3.7 convolution_convert_fusion.4
  991.8 10.0 convolution_convert_fusion.7
  1007.7 10.1 convolution_convert_fusion.2
  1018.1 10.1 convolution_convert_fusion.1
  1028.3 10.1 convolution_convert_fusion
  1042.1 16.6 %reduce-scatter.14.cloned.1.call-done = bf16[256,512]{1,0:T(8,128)(2,1)} async-done(((bf16[2048,512]{1,0:T(8,128)(2,1)}), bf16[256,512]{1,0:T(8,128)(2,1)}) %reduce-scatter.14.cloned.1.call-update) | async-done | bytes 262160 | tf_op jit(solution)/shard_map/reduce_scatter | solution.py:319
  1060.5 34.7 %reduce-scatter.16.cloned.1.call-done = bf16[256,512]{1,0:T(8,128)(2,1)} async-done(((bf16[2048,512]{1,0:T(8,128)(2,1)}), bf16[256,512]{1,0:T(8,128)(2,1)}) %reduce-scatter.16.cloned.1.call-update) | async-done | bytes 262160 | tf_op jit(solution)/shard_map/reduce_scatter | solution.py:322
  1097.1 34.9 %reduce-scatter.18.cloned.1.call-done = bf16[256,512]{1,0:T(8,128)(2,1)} async-done(((bf16[2048,512]{1,0:T(8,128)(2,1)}), bf16[256,512]{1,0:T(8,128)(2,1)}) %reduce-scatter.18.cloned.1.call-update) | async-done | bytes 262160 | tf_op jit(solution)/shard_map/reduce_scatter | solution.py:325
  1133.8 105.0 %all-reduce.12.cloned.1.call-done = (bf16[512,2048]{1,0:T(8,128)(2,1)}, bf16[512,2048]{1,0:T(8,128)(2,1)}) async-done(((bf16[512,2048]{1,0:T(8,128)(2,1)}, bf16[512,2048]{1,0:T(8,128)(2,1)}), (bf16[512,2048]{1,0:T(8,128)(2,1)}, bf16[512,2048]{1,0:T(8,128)(2,1)})) %all-reduce.12.cloned.1.call-update) | async-done | bytes 4194320 | tf_op jit(solution)/shard_map/psum | solution.py:189
  1238.8 3.2 fusion.30
  1241.9 17.2 %all-reduce.2 = (bf16[2048]{0:T(1024)(128)(2,1)S(1)}, bf16[2048]{0:T(1024)(128)(2,1)S(1)}) all-reduce(bf16[2048]{0:T(1024)(128)(2,1)S(1)} %get-tuple-element.137, bf16[2048]{0:T(1024)(128)(2,1)S(1)} %get-tuple-element.135), channel_id=4, replica_groups=mesh['seq'=8,'tp'=4] {'seq'}, use_global_device_ids=true, to_apply=%region_15.16.clone | all-reduce | flops 4096 | bytes 16384
  1260.4 5.1 add_convert_fusion.2
  1265.6 3.2 fusion.18
  1268.8 62.6 %reduce-scatter.22.cloned.1.call-done = bf16[256,2048]{1,0:T(8,128)(2,1)} async-done(((bf16[2048,2048]{1,0:T(8,128)(2,1)}), bf16[256,2048]{1,0:T(8,128)(2,1)}) %reduce-scatter.22.cloned.1.call-update) | async-done | bytes 1048592 | tf_op jit(solution)/shard_map/reduce_scatter | solution.py:331
  1334.1 87.3 %reduce-scatter.24.cloned.1.call-done = bf16[256,2048]{1,0:T(8,128)(2,1)} async-done(((bf16[2048,2048]{1,0:T(8,128)(2,1)}), bf16[256,2048]{1,0:T(8,128)(2,1)}) %reduce-scatter.24.cloned.1.call-update) | async-done | bytes 1048592 | tf_op jit(solution)/shard_map/reduce_scatter | solution.py:334
  1424.2 87.6 %reduce-scatter.26.cloned.1.call-done = bf16[2048,256]{1,0:T(8,128)(2,1)} async-done(((bf16[2048,2048]{1,0:T(8,128)(2,1)}), bf16[2048,256]{1,0:T(8,128)(2,1)}) %reduce-scatter.26.cloned.1.call-update) | async-done | bytes 1048592 | tf_op jit(solution)/shard_map/reduce_scatter | solution.py:337
  (370 shorter events, 234.4 us)
Async XLA Ops:
  7.2 8.0 copy-start.5
  7.2 34.9 %copy-start.29 = (f32[2048]{0:T(1024)S(1)}, f32[2048]{0:T(1024)}, u32[]{:S(2)}) copy-start(f32[2048]{0:T(1024)} %param.18) | copy-start | bytes 24580
  7.2 34.8 %all-gather.17.cloned.1.call-start = ((), (), s32[]{:S(2)}) async-start(), calls=%async_computation.12 | async-start | bytes 2359296 | tf_op jit(solution)/shard_map/all_gather | solution.py:138
  9.2 63.7 %all-gather.15.cloned.1.call-start = ((), (), s32[]{:S(2)}) async-start(), calls=%async_computation.11 | async-start | bytes 2359296 | tf_op jit(solution)/shard_map/all_gather | solution.py:137
  11.0 92.6 %all-gather.11.cloned.1.call-start = ((), (), s32[]{:S(2)}) async-start(), calls=%async_computation.9 | async-start | bytes 2359296 | tf_op jit(solution)/shard_map/all_gather | solution.py:139
  12.9 139.5 %all-gather.19.cloned.1.call-start = ((), (), s32[]{:S(2)}) async-start(), calls=%async_computation.13 | async-start | bytes 4718592 | tf_op jit(solution)/shard_map/all_gather | solution.py:164
  16.2 87.4 %copy-start.31 = (f32[512]{0:T(512)}, f32[512]{0:T(512)S(1)}, u32[]{:S(2)}) copy-start(f32[512]{0:T(512)S(1)} %get-tuple-element.187) | copy-start | bytes 6148
  16.8 59.0 %copy-start.20 = (f32[512,64]{0,1:T(8,128)}, f32[512,64]{0,1:T(8,128)S(1)}, u32[]{:S(2)}) copy-start(f32[512,64]{0,1:T(8,128)S(1)} %get-tuple-element.184) | copy-start | bytes 393220
  16.8 59.0 %copy-start.22 = (f32[512,64]{0,1:T(8,128)}, f32[512,64]{0,1:T(8,128)S(1)}, u32[]{:S(2)}) copy-start(f32[512,64]{0,1:T(8,128)S(1)} %get-tuple-element.185) | copy-start | bytes 393220
  79.1 32.9 %copy-start.26 = (s32[512]{0:T(512)S(1)}, s32[512]{0:T(512)}, u32[]{:S(2)}) copy-start(s32[512]{0:T(512)} %param.16) | copy-start | bytes 6148
  79.1 121.3 %all-gather.13.cloned.1.call-start = ((), (), s32[]{:S(2)}) async-start(), calls=%async_computation.10 | async-start | bytes 4718592 | tf_op jit(solution)/shard_map/all_gather | solution.py:165
  107.3 21.1 %copy-start.25 = (bf16[512,4,64]{0,2,1:T(8,128)(2,1)S(1)}, bf16[512,4,64]{0,2,1:T(8,128)(2,1)}, u32[]{:S(2)}) copy-start(bf16[512,4,64]{0,2,1:T(8,128)(2,1)} %get-tuple-element.174) | copy-start | bytes 786436
  107.3 21.5 %copy-start.24 = (bf16[512,4,64]{0,2,1:T(8,128)(2,1)S(1)}, bf16[512,4,64]{0,2,1:T(8,128)(2,1)}, u32[]{:S(2)}) copy-start(bf16[512,4,64]{0,2,1:T(8,128)(2,1)} %get-tuple-element.175) | copy-start | bytes 786436
  110.1 138.4 %all-gather.21.cloned.1.call-start = ((), (), s32[]{:S(2)}) async-start(), calls=%async_computation.14 | async-start | bytes 2359296 | tf_op jit(solution)/shard_map/all_gather | solution.py:140
  111.9 244.4 %all-reduce.8.cloned.1.call-start = ((), (), s32[]{:S(2)}) async-start(), calls=%async_computation.15 | async-start | bytes 8388608 | tf_op jit(solution)/shard_map/psum | solution.py:180
  112.5 520.4 %copy-start.28 = (s32[4,128]{1,0:T(4,128)}, s32[4,128]{1,0:T(4,128)S(1)}, u32[]{:S(2)}) copy-start(s32[4,128]{1,0:T(4,128)S(1)} %gather_fusion.1) | copy-start | bytes 6148
  248.4 5.1 copy-start.18
  253.5 187.1 %all-gather.23.cloned.1.call-start = ((), (), s32[]{:S(2)}) async-start(), calls=%async_computation.16 | async-start | bytes 9437184 | tf_op jit(solution)/shard_map/all_gather | solution.py:141
  256.3 267.2 %all-gather.25.cloned.1.call-start = ((), (), s32[]{:S(2)}) async-start(), calls=%async_computation.17 | async-start | bytes 9437184 | tf_op jit(solution)/shard_map/all_gather | solution.py:142
  259.3 347.4 %all-gather.27.cloned.1.call-start = ((), (), s32[]{:S(2)}) async-start(), calls=%async_computation.18 | async-start | bytes 9437184 | tf_op jit(solution)/shard_map/all_gather | solution.py:143
  262.0 99.1 %copy-start.27 = (f32[2048]{0:T(1024)S(1)}, f32[2048]{0:T(1024)}, u32[]{:S(2)}) copy-start(f32[2048]{0:T(1024)} %param.19) | copy-start | bytes 24580
  262.1 438.8 %all-reduce.10.cloned.1.call-start = ((), (), s32[]{:S(2)}) async-start(), calls=%async_computation.19 | async-start | bytes 4194304 | tf_op jit(solution)/shard_map/psum | solution.py:208
  359.1 2.0 copy-start
  361.5 162.0 %copy-start.12 = (bf16[512,2048]{1,0:T(8,128)(2,1)}, bf16[512,2048]{1,0:T(8,128)(2,1)S(1)}, u32[]{:S(2)}) copy-start(bf16[512,2048]{1,0:T(8,128)(2,1)S(1)} %multiply_convert_fusion.3) | copy-start | bytes 6291460
  618.5 8.5 copy-start.37
  618.5 8.5 copy-start.36
  618.5 8.5 copy-start.34
  632.8 302.1 %reduce-scatter.10.cloned.1.call-start = ((), (), s32[]{:S(2)}) async-start(), calls=%async_computation.20 | async-start | bytes 4718592 | tf_op jit(solution)/shard_map/reduce_scatter | solution.py:279
  654.6 50.5 %copy-start.15 = (bf16[512,2048]{1,0:T(8,128)(2,1)S(1)}, bf16[512,2048]{1,0:T(8,128)(2,1)}, u32[]{:S(2)}) copy-start(bf16[512,2048]{1,0:T(8,128)(2,1)} %param.27) | copy-start | bytes 6291460
  700.8 4.4 copy-start.1
  700.8 4.7 copy-start.9
  705.6 3.3 copy-start.14
  706.8 2.0 copy-start.7
  727.8 2.7 copy-start.3
  748.3 2.7 copy-start.3
  770.1 2.7 copy-start.3
  791.8 2.7 copy-start.3
  813.6 2.7 copy-start.3
  835.3 2.7 copy-start.3
  857.0 2.7 copy-start.3
  878.8 2.8 copy-start.3
  884.7 1.2 copy-start.19
  884.7 100.7 %reduce-scatter.12.cloned.1.call-start = ((), (), s32[]{:S(2)}) async-start(), calls=%async_computation.21 | async-start | bytes 4718592 | tf_op jit(solution)/shard_map/reduce_scatter | solution.py:282
  885.5 5.3 copy-start.4
  885.5 154.9 %reduce-scatter.20.cloned.1.call-start = ((), (), s32[]{:S(2)}) async-start(), calls=%async_computation.25 | async-start | bytes 2359296 | tf_op jit(solution)/shard_map/reduce_scatter | solution.py:328
  890.7 168.0 %reduce-scatter.14.cloned.1.call-start = ((), (), s32[]{:S(2)}) async-start(), calls=%async_computation.22 | async-start | bytes 2359296 | tf_op jit(solution)/shard_map/reduce_scatter | solution.py:319
  937.0 6.8 copy-start.21
  937.1 6.8 copy-start.23
  939.0 6.5 copy-start.6
  939.0 6.5 copy-start.30
  939.0 6.5 copy-start.32
  948.3 147.0 %reduce-scatter.16.cloned.1.call-start = ((), (), s32[]{:S(2)}) async-start(), calls=%async_computation.23 | async-start | bytes 2359296 | tf_op jit(solution)/shard_map/reduce_scatter | solution.py:322
  951.2 180.8 %reduce-scatter.18.cloned.1.call-start = ((), (), s32[]{:S(2)}) async-start(), calls=%async_computation.24 | async-start | bytes 2359296 | tf_op jit(solution)/shard_map/reduce_scatter | solution.py:325
  991.6 247.2 %all-reduce.12.cloned.1.call-start = ((), (), s32[]{:S(2)}) async-start(), calls=%async_computation.29 | async-start | bytes 8388608 | tf_op jit(solution)/shard_map/psum | solution.py:189
  991.8 10.0 copy-start.16
  1001.8 1.6 copy-start.17
  1003.4 1.6 copy-start.11
  1003.4 1.7 copy-start.13
  1007.7 323.7 %reduce-scatter.22.cloned.1.call-start = ((), (), s32[]{:S(2)}) async-start(), calls=%async_computation.26 | async-start | bytes 9437184 | tf_op jit(solution)/shard_map/reduce_scatter | solution.py:331
  1017.9 403.5 %reduce-scatter.24.cloned.1.call-start = ((), (), s32[]{:S(2)}) async-start(), calls=%async_computation.27 | async-start | bytes 9437184 | tf_op jit(solution)/shard_map/reduce_scatter | solution.py:334
  1028.2 483.6 %reduce-scatter.26.cloned.1.call-start = ((), (), s32[]{:S(2)}) async-start(), calls=%async_computation.28 | async-start | bytes 9437184 | tf_op jit(solution)/shard_map/reduce_scatter | solution.py:337
  1260.4 5.1 copy-start.8
  1260.4 5.1 copy-start.10
  1260.4 5.1 copy-start.33
  (9 other events, 7.0 us)
Sparse Core Ops, SparseCore 0:
  10.2 31.7 all-gather.16
  44.2 28.5 all-gather.14
  75.0 28.5 all-gather.10
  105.7 46.6 all-gather.18
  154.4 45.9 all-gather.12
  202.4 29.5 all-gather.20
  253.7 102.5 all-reduce.7
  358.5 82.0 all-gather.22
  442.9 80.5 all-gather.24
  525.6 81.0 all-gather.26
  633.0 67.8 all-reduce.9
  884.8 50.0 reduce-scatter.9
  937.2 48.1 reduce-scatter.11
  987.5 33.9 reduce-scatter.19
  1024.3 34.4 reduce-scatter.13
  1060.9 34.3 reduce-scatter.15
  1097.4 34.5 reduce-scatter.17
  1135.9 102.8 all-reduce.11
  1241.2 90.1 reduce-scatter.21
  1333.6 87.7 reduce-scatter.23
  1423.8 87.9 reduce-scatter.25
where the time goes:
time: 1530 us; the launch traced here: 1520 us
  waiting for transfers between devices  986 us (64%)
  local copies, waits for them, and re-layouts  210 us (14%)
  matrix products  195 us (13%)
  other arithmetic  81.9 us (5%)
  blocking collectives  30.6 us (2%)
  between operations  15.9 us (1%)
    psum x1, waiting for transfers between devices, on_device(): lax.psum(matrix(hidden, down_full).astype(jnp.bfloat16), 'tp')  105 us
    psum x1, waiting for transfers between devices, on_device(): residual = inputs + lax.psum(matrix(mixed_heads, out_full), 'tp')  94 us
    reduce_scatter x1, waiting for transfers between devices, on_device(): lax.psum_scatter(grad_w_down.astype(jnp.bfloat16), 'seq', scatter_dimensi...  87.6 us
    reduce_scatter x1, waiting for transfers between devices, on_device(): lax.psum_scatter(grad_w_up.astype(jnp.bfloat16), 'seq', scatter_dimension...  87.3 us
    all_gather x1, waiting for transfers between devices, on_device(): lax.all_gather(w_gate.astype(jnp.bfloat16), 'seq', axis=0, tiled=True)  79.1 us
    all_gather x1, waiting for transfers between devices, on_device(): lax.all_gather(w_down.astype(jnp.bfloat16), 'seq', axis=1, tiled=True)  73.7 us
    all_gather x1, waiting for transfers between devices, on_device(): lax.all_gather(w_up.astype(jnp.bfloat16), 'seq', axis=0, tiled=True)  73.5 us
    reduce_scatter x1, waiting for transfers between devices, on_device(): lax.psum_scatter(grad_w_gate.astype(jnp.bfloat16), 'seq', scatter_dimensi...  62.6 us
  transfers between devices with their start and end apart: 21, of which 19 were waited for; matrix products, arithmetic and copies ran while one was open for 17% of the time, Pallas kernels for 0%

commit v1 on v0

--- a/solution.py
+++ b/solution.py
@@ -3,6 +3,7 @@
 import jax.numpy as jnp
 from jax import lax
 from jax.sharding import PartitionSpec as P
+from jax.lax import all_gather
 
 HD = 128
 EPSILON = 1e-06
@@ -161,8 +162,9 @@
     query_split = regroup(query_sorted, row_count)
     qpos_split = regroup(pos_sorted, row_count)
     zero_out = jnp.zeros((row_count, head_count, HD), jnp.float32)
-    key_block = lax.all_gather(key_rows, "seq", axis=0, tiled=True)
-    value_block = lax.all_gather(value_sorted, "seq", axis=0, tiled=True)
+    fresh = jnp.concatenate([key_rows, value_sorted], 1)
+    main = all_gather(fresh, "seq", axis=0, tiled=True)
+    key_block, value_block = jnp.split(main, [key_rows.shape[1]], 1)
     piece_rows = key_block.shape[0]
     key_pos = every_pos
     key_heads_piece = key_block.reshape(piece_rows, head_count, HD)

time: 1530 us -> 1630 us (1.065)
  waiting for transfers between devices: 986 us -> 1070 us
    all_gather x2 -> x3, waiting for transfers between devices: 43.5 us -> 108 us  [the longest x1 54.3 us: on_device(): main = all_gather(fresh, 'seq', axis=0, tiled=True)]
    psum x1, waiting for transfers between devices: 38.2 us -> 57.9 us  [on_device(): lax.psum((outer_cols(grad_gate, gate_full) + outer_cols(grad_up, up_full)...]
  transfers between devices with their start and end apart: 21 -> 22, of which waited for: 19 -> 20; matrix products, arithmetic and copies ran while one was open for 17% -> 18% of each run, Pallas kernels for 0% -> 0%
where the time goes in v1:
time: 1630 us; the launch traced here: 1620 us
  waiting for transfers between devices  1070 us (66%)
  local copies, waits for them, and re-layouts  219 us (13%)
  matrix products  194 us (12%)
  other arithmetic  84.4 us (5%)
  blocking collectives  30.7 us (2%)
    psum x1, waiting for transfers between devices, on_device(): lax.psum(matrix(hidden, down_full).astype(jnp.bfloat16), 'tp')  105 us
    psum x1, waiting for transfers between devices, on_device(): residual = inputs + lax.psum(matrix(mixed_heads, out_full), 'tp')  92.2 us
    reduce_scatter x1, waiting for transfers between devices, on_device(): lax.psum_scatter(grad_w_down.astype(jnp.bfloat16), 'seq', scatter_dimensi...  87.6 us
    reduce_scatter x1, waiting for transfers between devices, on_device(): lax.psum_scatter(grad_w_up.astype(jnp.bfloat16), 'seq', scatter_dimension...  87.4 us
    all_gather x1, waiting for transfers between devices, on_device(): lax.all_gather(w_gate.astype(jnp.bfloat16), 'seq', axis=0, tiled=True)  79.1 us
    all_gather x1, waiting for transfers between devices, on_device(): lax.all_gather(w_down.astype(jnp.bfloat16), 'seq', axis=1, tiled=True)  73.9 us
    all_gather x1, waiting for transfers between devices, on_device(): lax.all_gather(w_up.astype(jnp.bfloat16), 'seq', axis=0, tiled=True)  73.5 us
    reduce_scatter x1, waiting for transfers between devices, on_device(): lax.psum_scatter(grad_w_gate.astype(jnp.bfloat16), 'seq', scatter_dimensi...  62.4 us
  transfers between devices with their start and end apart: 22, of which 20 were waited for; matrix products, arithmetic and copies ran while one was open for 18% of the time, Pallas kernels for 0%

profile of v1, /device:TPU:0, one launch (start us, length us, event | category | flops | bytes accessed | tf_op | source)
XLA Modules:
  0.0 1618.0 jit_solution(8736320568862244404)
XLA Ops:
  16.9 25.2 %all-gather.12.cloned.1.call-done = bf16[2048,512]{1,0:T(8,128)(2,1)} async-done(((bf16[256,512]{1,0:T(8,128)(2,1)}), bf16[2048,512]{1,0:T(8,128)(2,1)}) %all-gather.12.cloned.1.call-update) | async-done | bytes 2097168 | tf_op jit(solution)/shard_map/all_gather | solution.py:139
  42.0 3.0 fusion.53
  45.0 27.8 %all-gather.18.cloned.1.call-done = bf16[2048,512]{1,0:T(8,128)(2,1)} async-done(((bf16[256,512]{1,0:T(8,128)(2,1)}), bf16[2048,512]{1,0:T(8,128)(2,1)}) %all-gather.18.cloned.1.call-update) | async-done | bytes 2097168 | tf_op jit(solution)/shard_map/all_gather | solution.py:138
  72.8 3.0 fusion.50
  78.3 25.4 %all-gather.14.cloned.1.call-done = bf16[2048,512]{1,0:T(8,128)(2,1)} async-done(((bf16[256,512]{1,0:T(8,128)(2,1)}), bf16[2048,512]{1,0:T(8,128)(2,1)}) %all-gather.14.cloned.1.call-update) | async-done | bytes 2097168 | tf_op jit(solution)/shard_map/all_gather | solution.py:140
  103.7 2.9 convolution_convert_fusion.9
  112.9 13.4 all-gather
  137.8 54.3 %all-gather.16.cloned.1.call-done = bf16[4096,1024]{0,1:T(8,128)(2,1)} async-done(((bf16[512,1024]{0,1:T(8,128)(2,1)}), bf16[4096,1024]{0,1:T(8,128)(2,1)}) %all-gather.16.cloned.1.call-update) | async-done | bytes 8388624 | tf_op jit(solution)/shard_map/all_gather | solution.py:166
  192.1 6.1 fusion.55
  198.2 7.8 reshape.325
  206.0 11.8 copy.120
  217.8 6.3 copy.96
  224.1 7.4 reshape.217
  231.5 7.8 reshape.326
  239.3 11.8 copy.121
  251.1 5.3 copy.101
  256.4 10.7 fusion.33
  271.3 5.0 fusion.37
  279.2 3.1 convert_element_type.200
  286.6 92.2 %all-reduce.8.cloned.1.call-done = f32[512,2048]{1,0:T(8,128)} async-done(((f32[512,2048]{1,0:T(8,128)}), f32[512,2048]{1,0:T(8,128)}) %all-reduce.8.cloned.1.call-update) | async-done | bytes 4194320 | tf_op jit(solution)/shard_map/psum | solution.py:182
  384.1 79.1 %all-gather.22.cloned.1.call-done = bf16[2048,2048]{1,0:T(8,128)(2,1)} async-done(((bf16[256,2048]{1,0:T(8,128)(2,1)}), bf16[2048,2048]{1,0:T(8,128)(2,1)}) %all-gather.22.cloned.1.call-update) | async-done | bytes 8388624 | tf_op jit(solution)/shard_map/all_gather | solution.py:142
  463.2 9.4 fusion.57
  472.6 73.5 %all-gather.24.cloned.1.call-done = bf16[2048,2048]{1,0:T(8,128)(2,1)} async-done(((bf16[256,2048]{1,0:T(8,128)(2,1)}), bf16[2048,2048]{1,0:T(8,128)(2,1)}) %all-gather.24.cloned.1.call-update) | async-done | bytes 8388624 | tf_op jit(solution)/shard_map/all_gather | solution.py:143
  546.1 9.4 fusion.58
  555.5 73.9 %all-gather.26.cloned.1.call-done = bf16[2048,2048]{1,0:T(8,128)(2,1)} async-done(((bf16[2048,256]{1,0:T(8,128)(2,1)}), bf16[2048,2048]{1,0:T(8,128)(2,1)}) %all-gather.26.cloned.1.call-update) | async-done | bytes 8388624 | tf_op jit(solution)/shard_map/all_gather | solution.py:144
  629.4 11.8 multiply_convert_fusion
  641.2 8.5 fusion.59
  649.8 5.8 add_convert_fusion.1
  656.5 20.4 %all-gather.28.cloned.1.call-done = bf16[4096,512]{0,1:T(8,128)(2,1)} async-done(((bf16[512,512]{0,1:T(8,128)(2,1)}), bf16[4096,512]{0,1:T(8,128)(2,1)}) %all-gather.28.cloned.1.call-update) | async-done | bytes 4194320 | tf_op jit(solution)/shard_map/all_gather | solution.py:230
  676.9 6.3 copy.127
  683.3 8.3 copy.108
  691.5 33.6 %all-gather.30.cloned.1.call-done = bf16[4096,512]{0,1:T(8,128)(2,1)} async-done(((bf16[512,512]{0,1:T(8,128)(2,1)}), bf16[4096,512]{0,1:T(8,128)(2,1)}) %all-gather.30.cloned.1.call-update) | async-done | bytes 4194320 | tf_op jit(solution)/shard_map/all_gather | solution.py:231
  725.1 6.4 copy.128
  731.5 8.0 copy.109
  739.5 57.9 %all-reduce.10.cloned.1.call-done = bf16[512,2048]{1,0:T(8,128)(2,1)} async-done(((bf16[512,2048]{1,0:T(8,128)(2,1)}), bf16[512,2048]{1,0:T(8,128)(2,1)}) %all-reduce.10.cloned.1.call-update) | async-done | bytes 2097168 | tf_op jit(solution)/shard_map/psum | solution.py:210
  797.3 4.3 fusion.23
  808.4 172.8 %while.16 = (s32[]{:T(128)}, f32[512,4,128]{2,0,1:T(8,128)}, bf16[8,512,512]{2,1,0:T(8,128)(2,1)}, bf16[8,512,512]{2,1,0:T(8,128)(2,1)}, bf16[8,512,4,128]{3,1,2...) while((s32[]{:T(128)}, f32[512,4,128]{2,0,1:T(8,128)}, ...), condition=%wide.wide.region_9.10_spmd.clone, body=%wide.wide.region_8.9_spmd.clone.sunk | while | flops 678297600 | bytes 37630664 | solution.py:277
  810.3 3.1 add_divide_fusion.4
  830.8 3.1 add_divide_fusion.4
  852.5 3.1 add_divide_fusion.4
  874.2 3.1 add_divide_fusion.4
  896.0 3.1 add_divide_fusion.4
  917.7 3.1 add_divide_fusion.4
  939.4 3.1 add_divide_fusion.4
  961.2 3.1 add_divide_fusion.4
  982.2 4.8 convolution_convert_fusion.3
  988.6 42.8 %reduce-scatter.10.cloned.1.call-done = bf16[512,512]{1,0:T(8,128)(2,1)} async-done(((bf16[4096,512]{1,0:T(8,128)(2,1)}), bf16[512,512]{1,0:T(8,128)(2,1)}) %reduce-scatter.10.cloned.1.call-update) | async-done | bytes 524304 | tf_op jit(solution)/shard_map/reduce_scatter | solution.py:281
  1047.7 34.0 %reduce-scatter.12.cloned.1.call-done = bf16[512,512]{1,0:T(8,128)(2,1)} async-done(((bf16[4096,512]{1,0:T(8,128)(2,1)}), bf16[512,512]{1,0:T(8,128)(2,1)}) %reduce-scatter.12.cloned.1.call-update) | async-done | bytes 524304 | tf_op jit(solution)/shard_map/reduce_scatter | solution.py:284
  1084.1 3.8 convolution_convert_fusion.4
  1088.1 10.0 convolution_convert_fusion.7
  1104.1 10.1 convolution_convert_fusion.2
  1114.5 10.1 convolution_convert_fusion.1
  1124.6 10.1 convolution_convert_fusion
  1138.5 16.5 %reduce-scatter.14.cloned.1.call-done = bf16[256,512]{1,0:T(8,128)(2,1)} async-done(((bf16[2048,512]{1,0:T(8,128)(2,1)}), bf16[256,512]{1,0:T(8,128)(2,1)}) %reduce-scatter.14.cloned.1.call-update) | async-done | bytes 262160 | tf_op jit(solution)/shard_map/reduce_scatter | solution.py:321
  1156.7 34.8 %reduce-scatter.16.cloned.1.call-done = bf16[256,512]{1,0:T(8,128)(2,1)} async-done(((bf16[2048,512]{1,0:T(8,128)(2,1)}), bf16[256,512]{1,0:T(8,128)(2,1)}) %reduce-scatter.16.cloned.1.call-update) | async-done | bytes 262160 | tf_op jit(solution)/shard_map/reduce_scatter | solution.py:324
  1193.3 34.9 %reduce-scatter.18.cloned.1.call-done = bf16[256,512]{1,0:T(8,128)(2,1)} async-done(((bf16[2048,512]{1,0:T(8,128)(2,1)}), bf16[256,512]{1,0:T(8,128)(2,1)}) %reduce-scatter.18.cloned.1.call-update) | async-done | bytes 262160 | tf_op jit(solution)/shard_map/reduce_scatter | solution.py:327
  1230.0 105.1 %all-reduce.12.cloned.1.call-done = (bf16[512,2048]{1,0:T(8,128)(2,1)}, bf16[512,2048]{1,0:T(8,128)(2,1)}) async-done(((bf16[512,2048]{1,0:T(8,128)(2,1)}, bf16[512,2048]{1,0:T(8,128)(2,1)}), (bf16[512,2048]{1,0:T(8,128)(2,1)}, bf16[512,2048]{1,0:T(8,128)(2,1)})) %all-reduce.12.cloned.1.call-update) | async-done | bytes 4194320 | tf_op jit(solution)/shard_map/psum | solution.py:191
  1335.2 3.2 fusion.30
  1338.3 17.3 %all-reduce.2 = (bf16[2048]{0:T(1024)(128)(2,1)S(1)}, bf16[2048]{0:T(1024)(128)(2,1)S(1)}) all-reduce(bf16[2048]{0:T(1024)(128)(2,1)S(1)} %get-tuple-element.137, bf16[2048]{0:T(1024)(128)(2,1)S(1)} %get-tuple-element.135), channel_id=4, replica_groups=mesh['seq'=8,'tp'=4] {'seq'}, use_global_device_ids=true, to_apply=%region_15.16.clone | all-reduce | flops 4096 | bytes 16384
  1356.9 5.1 add_convert_fusion.2
  1362.0 3.2 fusion.18
  1365.2 62.4 %reduce-scatter.22.cloned.1.call-done = bf16[256,2048]{1,0:T(8,128)(2,1)} async-done(((bf16[2048,2048]{1,0:T(8,128)(2,1)}), bf16[256,2048]{1,0:T(8,128)(2,1)}) %reduce-scatter.22.cloned.1.call-update) | async-done | bytes 1048592 | tf_op jit(solution)/shard_map/reduce_scatter | solution.py:333
  1430.4 87.4 %reduce-scatter.24.cloned.1.call-done = bf16[256,2048]{1,0:T(8,128)(2,1)} async-done(((bf16[2048,2048]{1,0:T(8,128)(2,1)}), bf16[256,2048]{1,0:T(8,128)(2,1)}) %reduce-scatter.24.cloned.1.call-update) | async-done | bytes 1048592 | tf_op jit(solution)/shard_map/reduce_scatter | solution.py:336
  1520.6 87.6 %reduce-scatter.26.cloned.1.call-done = bf16[2048,256]{1,0:T(8,128)(2,1)} async-done(((bf16[2048,2048]{1,0:T(8,128)(2,1)}), bf16[2048,256]{1,0:T(8,128)(2,1)}) %reduce-scatter.26.cloned.1.call-update) | async-done | bytes 1048592 | tf_op jit(solution)/shard_map/reduce_scatter | solution.py:339
  (375 shorter events, 246.9 us)
Async XLA Ops:
  7.2 8.0 copy-start.5
  7.2 34.9 %copy-start.29 = (f32[2048]{0:T(1024)S(1)}, f32[2048]{0:T(1024)}, u32[]{:S(2)}) copy-start(f32[2048]{0:T(1024)} %param.18) | copy-start | bytes 24580
  7.2 34.8 %all-gather.12.cloned.1.call-start = ((), (), s32[]{:S(2)}) async-start(), calls=%async_computation.9 | async-start | bytes 2359296 | tf_op jit(solution)/shard_map/all_gather | solution.py:139
  9.2 63.7 %all-gather.18.cloned.1.call-start = ((), (), s32[]{:S(2)}) async-start(), calls=%async_computation.12 | async-start | bytes 2359296 | tf_op jit(solution)/shard_map/all_gather | solution.py:138
  11.0 92.6 %all-gather.14.cloned.1.call-start = ((), (), s32[]{:S(2)}) async-start(), calls=%async_computation.10 | async-start | bytes 2359296 | tf_op jit(solution)/shard_map/all_gather | solution.py:140
  12.9 179.2 %all-gather.16.cloned.1.call-start = ((), (), s32[]{:S(2)}) async-start(), calls=%async_computation.11 | async-start | bytes 9437184 | tf_op jit(solution)/shard_map/all_gather | solution.py:166
  16.3 87.3 %copy-start.31 = (f32[512]{0:T(512)}, f32[512]{0:T(512)S(1)}, u32[]{:S(2)}) copy-start(f32[512]{0:T(512)S(1)} %get-tuple-element.189) | copy-start | bytes 6148
  16.8 59.0 %copy-start.22 = (f32[512,64]{0,1:T(8,128)}, f32[512,64]{0,1:T(8,128)S(1)}, u32[]{:S(2)}) copy-start(f32[512,64]{0,1:T(8,128)S(1)} %get-tuple-element.186) | copy-start | bytes 393220
  16.9 59.0 %copy-start.24 = (f32[512,64]{0,1:T(8,128)}, f32[512,64]{0,1:T(8,128)S(1)}, u32[]{:S(2)}) copy-start(f32[512,64]{0,1:T(8,128)S(1)} %get-tuple-element.187) | copy-start | bytes 393220
  78.3 30.9 %copy-start.11 = (bf16[512,512]{0,1:T(8,128)(2,1)}, bf16[512,512]{0,1:T(8,128)(2,1)S(1)}, u32[]{:S(2)}) copy-start(bf16[512,512]{0,1:T(8,128)(2,1)S(1)} %copy.94) | copy-start | bytes 1572868
  106.5 5.7 copy-start.26
  109.2 25.1 %copy-start.12 = (bf16[512,512]{0,1:T(8,128)(2,1)}, bf16[512,512]{0,1:T(8,128)(2,1)S(1)}, u32[]{:S(2)}) copy-start(bf16[512,512]{0,1:T(8,128)(2,1)S(1)} %copy.119) | copy-start | bytes 1572868
  110.4 160.9 %all-gather.20.cloned.1.call-start = ((), (), s32[]{:S(2)}) async-start(), calls=%async_computation.13 | async-start | bytes 2359296 | tf_op jit(solution)/shard_map/all_gather | solution.py:141
  112.2 266.7 %all-reduce.8.cloned.1.call-start = ((), (), s32[]{:S(2)}) async-start(), calls=%async_computation.14 | async-start | bytes 8388608 | tf_op jit(solution)/shard_map/psum | solution.py:182
  112.8 542.8 %copy-start.28 = (s32[4,128]{1,0:T(4,128)}, s32[4,128]{1,0:T(4,128)S(1)}, u32[]{:S(2)}) copy-start(s32[4,128]{1,0:T(4,128)S(1)} %gather_fusion.2) | copy-start | bytes 6148
  271.3 5.1 copy-start.20
  276.4 186.9 %all-gather.22.cloned.1.call-start = ((), (), s32[]{:S(2)}) async-start(), calls=%async_computation.15 | async-start | bytes 9437184 | tf_op jit(solution)/shard_map/all_gather | solution.py:142
  279.2 267.0 %all-gather.24.cloned.1.call-start = ((), (), s32[]{:S(2)}) async-start(), calls=%async_computation.16 | async-start | bytes 9437184 | tf_op jit(solution)/shard_map/all_gather | solution.py:143
  282.4 347.1 %all-gather.26.cloned.1.call-start = ((), (), s32[]{:S(2)}) async-start(), calls=%async_computation.17 | async-start | bytes 9437184 | tf_op jit(solution)/shard_map/all_gather | solution.py:144
  285.1 391.8 %all-gather.28.cloned.1.call-start = ((), (), s32[]{:S(2)}) async-start(), calls=%async_computation.19 | async-start | bytes 4718592 | tf_op jit(solution)/shard_map/all_gather | solution.py:230
  285.7 439.4 %all-gather.30.cloned.1.call-start = ((), (), s32[]{:S(2)}) async-start(), calls=%async_computation.20 | async-start | bytes 4718592 | tf_op jit(solution)/shard_map/all_gather | solution.py:231
  286.4 97.3 %copy-start.27 = (f32[2048]{0:T(1024)S(1)}, f32[2048]{0:T(1024)}, u32[]{:S(2)}) copy-start(f32[2048]{0:T(1024)} %param.19) | copy-start | bytes 24580
  286.4 510.9 %all-reduce.10.cloned.1.call-start = ((), (), s32[]{:S(2)}) async-start(), calls=%async_computation.18 | async-start | bytes 4194304 | tf_op jit(solution)/shard_map/psum | solution.py:210
  381.7 2.0 copy-start
  384.1 162.0 %copy-start.14 = (bf16[512,2048]{1,0:T(8,128)(2,1)}, bf16[512,2048]{1,0:T(8,128)(2,1)S(1)}, u32[]{:S(2)}) copy-start(bf16[512,2048]{1,0:T(8,128)(2,1)S(1)} %multiply_convert_fusion.3) | copy-start | bytes 6291460
  641.2 8.6 copy-start.37
  641.2 8.6 copy-start.36
  641.2 8.6 copy-start.34
  655.6 375.8 %reduce-scatter.10.cloned.1.call-start = ((), (), s32[]{:S(2)}) async-start(), calls=%async_computation.21 | async-start | bytes 4718592 | tf_op jit(solution)/shard_map/reduce_scatter | solution.py:281
  731.5 70.2 %copy-start.17 = (bf16[512,2048]{1,0:T(8,128)(2,1)S(1)}, bf16[512,2048]{1,0:T(8,128)(2,1)}, u32[]{:S(2)}) copy-start(bf16[512,2048]{1,0:T(8,128)(2,1)} %param.27) | copy-start | bytes 6291460
  797.3 4.4 copy-start.1
  797.3 4.7 copy-start.9
  802.1 3.3 copy-start.16
  803.3 2.0 copy-start.7
  824.3 2.7 copy-start.3
  844.8 2.7 copy-start.3
  866.6 2.7 copy-start.3
  888.3 2.7 copy-start.3
  910.0 2.7 copy-start.3
  931.8 2.7 copy-start.3
  953.5 2.7 copy-start.3
  975.3 2.8 copy-start.3
  981.2 100.5 %reduce-scatter.12.cloned.1.call-start = ((), (), s32[]{:S(2)}) async-start(), calls=%async_computation.22 | async-start | bytes 4718592 | tf_op jit(solution)/shard_map/reduce_scatter | solution.py:284
  981.8 5.3 copy-start.4
  981.8 154.9 %reduce-scatter.20.cloned.1.call-start = ((), (), s32[]{:S(2)}) async-start(), calls=%async_computation.26 | async-start | bytes 2359296 | tf_op jit(solution)/shard_map/reduce_scatter | solution.py:330
  987.0 167.9 %reduce-scatter.14.cloned.1.call-start = ((), (), s32[]{:S(2)}) async-start(), calls=%async_computation.23 | async-start | bytes 2359296 | tf_op jit(solution)/shard_map/reduce_scatter | solution.py:321
  1033.5 6.8 copy-start.23
  1033.5 6.8 copy-start.25
  1035.4 6.5 copy-start.6
  1035.4 6.5 copy-start.30
  1035.5 6.5 copy-start.32
  1044.8 146.7 %reduce-scatter.16.cloned.1.call-start = ((), (), s32[]{:S(2)}) async-start(), calls=%async_computation.24 | async-start | bytes 2359296 | tf_op jit(solution)/shard_map/reduce_scatter | solution.py:324
  1047.7 180.5 %reduce-scatter.18.cloned.1.call-start = ((), (), s32[]{:S(2)}) async-start(), calls=%async_computation.25 | async-start | bytes 2359296 | tf_op jit(solution)/shard_map/reduce_scatter | solution.py:327
  1087.9 247.3 %all-reduce.12.cloned.1.call-start = ((), (), s32[]{:S(2)}) async-start(), calls=%async_computation.30 | async-start | bytes 8388608 | tf_op jit(solution)/shard_map/psum | solution.py:191
  1088.1 10.0 copy-start.18
  1098.1 1.6 copy-start.19
  1099.7 1.6 copy-start.13
  1099.7 1.7 copy-start.15
  1104.0 323.6 %reduce-scatter.22.cloned.1.call-start = ((), (), s32[]{:S(2)}) async-start(), calls=%async_computation.27 | async-start | bytes 9437184 | tf_op jit(solution)/shard_map/reduce_scatter | solution.py:333
  1114.2 403.6 %reduce-scatter.24.cloned.1.call-start = ((), (), s32[]{:S(2)}) async-start(), calls=%async_computation.28 | async-start | bytes 9437184 | tf_op jit(solution)/shard_map/reduce_scatter | solution.py:336
  1124.6 483.6 %reduce-scatter.26.cloned.1.call-start = ((), (), s32[]{:S(2)}) async-start(), calls=%async_computation.29 | async-start | bytes 9437184 | tf_op jit(solution)/shard_map/reduce_scatter | solution.py:339
  1356.9 5.1 copy-start.8
  1356.9 5.1 copy-start.10
  1356.9 5.1 copy-start.33
  (10 other events, 8.1 us)
Sparse Core Ops, SparseCore 0:
  10.2 31.7 all-gather.11
  44.2 28.5 all-gather.17
  75.0 28.5 all-gather.13
  110.5 81.5 all-gather.15
  194.1 29.3 all-gather.19
  276.5 102.3 all-reduce.7
  381.1 82.0 all-gather.21
  465.5 80.5 all-gather.23
  548.4 81.0 all-gather.25
  631.5 45.3 all-gather.27
  679.2 45.8 all-gather.29
  728.9 68.3 all-reduce.9
  981.3 49.9 reduce-scatter.9
  1033.5 48.1 reduce-scatter.11
  1083.8 34.0 reduce-scatter.19
  1120.6 34.2 reduce-scatter.13
  1157.1 34.4 reduce-scatter.15
  1193.7 34.5 reduce-scatter.17
  1232.3 102.8 all-reduce.11
  1337.4 90.1 reduce-scatter.21
  1430.0 87.7 reduce-scatter.23
  1520.2 87.9 reduce-scatter.25
